TPU v7x, 256 devices: a whole 4x4x8 slice. The times are simulated.
256 devices in a mesh: seq: 8 (over y, core), tensor: 32 (over z, x).
Axes of the slice: x: 4, y: 4, z: 8, core: 2. Of those that a mesh axis runs over, the one named last changes fastest.
Arguments:
- tokens: bfloat16 [4096, 3584], P('seq', 'tensor'), may hold values from -6 to 6
- w_zx: bfloat16 [2, 3584, 4096], P(None, None, 'tensor'), may hold values from -0.09375 to 0.09375
- w_bc: bfloat16 [3584, 128], replicated, may hold values from -0.09375 to 0.09375
- w_dt: bfloat16 [3584, 64], P(None, 'tensor'), may hold values from -0.09375 to 0.09375
- dt_bias: float32 [64], P('tensor'), may hold values from -2 to 0.5
- a_rate: float32 [64], P('tensor'), may hold values from 0.00012207031 to 0.05
- d_skip: float32 [64], P('tensor'), may hold values from 0.3 to 1.5
- conv_x: float32 [4, 4096], P(None, 'tensor'), may hold values from -3 to 3
- conv_bc: float32 [4, 128], replicated, may hold values from -3 to 3
- norm_gain: float32 [4096], P('tensor'), may hold values from 0.25 to 1.75
- w_out: bfloat16 [4096, 3584], P('tensor'), may hold values from -0.09375 to 0.09375
- segments: int32 [4096], P('seq'), may hold values from 0 to 5, never falling along the last dimension, each value on 1 to 2048 neighbouring positions
Outputs:
- mixed: bfloat16 [4096, 3584], P(('seq', 'tensor'))
Inputs may be any that keep to these rules, and one draw needn't show every extreme that they name: `segments`: prompt ids never fall along the tokens, so each prompt's tokens are contiguous.
All inputs are finite; a program needn't handle non-finite values.
Results may differ from a plain program's by a relative error of at most 0.02.
Values may be sent and summed in bfloat16 or wider, within the bound.
A program may use at most 64 MiB of HBM per device.

v0:
```python
import jax
import jax.numpy as jnp
from jax import lax
from jax.sharding import PartitionSpec as P

BLOCK = 256


HIGHEST_PREC = lax.Precision.HIGHEST
NORM_EPS = 1e-05


def from_behind(block, axis, distance):
    devices = range(lax.axis_size(axis))
    route = [(i - distance, i) for i in devices if i - distance in devices]
    return lax.ppermute(block, axis, route)


def entering(array, axis, join, neutral):
    place = lax.axis_index(axis)
    gathered = jax.tree.map(
        lambda a, kind: lax.all_gather(a.astype(kind), axis),
        array,
        jax.tree.map(lambda a: jnp.bfloat16 if a.dtype == jnp.float32 else a.dtype, array),
    )
    state = jax.tree.map(lambda a, e: jnp.zeros_like(a) + jnp.asarray(e, a.dtype), array, neutral)

    def one(turn, state):
        return join(
            state,
            jax.tree.map(
                lambda a, own: lax.dynamic_index_in_dim(a, turn, 0, False).astype(own.dtype),
                gathered,
                array,
            ),
        )

    return lax.fori_loop(0, place, one, state)


def conv_tail(extended, seg_ext, taps, tok_rows):
    conv_len = taps.shape[0]
    seg_now = seg_ext[conv_len - 1 :]
    conv_sum = taps[conv_len - 1] * extended[conv_len - 1 :]
    for offset in range(1, conv_len):
        earlier = extended[conv_len - 1 - offset : conv_len - 1 - offset + tok_rows]
        seg_then = seg_ext[conv_len - 1 - offset : conv_len - 1 - offset + tok_rows]
        conv_sum = conv_sum + taps[conv_len - 1 - offset] * jnp.where(
            (seg_then == seg_now)[:, None], earlier, 0.0
        )
    return jax.nn.silu(conv_sum)


def ssd_block(carry, block):
    state, last_seg = carry
    inner_x, step_size, logdec, bmat, cmat, seg_ids = block
    cum_decay = jnp.cumsum(logdec, axis=0)
    position = jnp.arange(seg_ids.shape[0])
    visible = (seg_ids[:, None] == seg_ids[None, :]) & (position[:, None] >= position[None, :])
    gap_decay = jnp.where(
        visible[:, :, None], cum_decay[:, None, :] - cum_decay[None, :, :], -jnp.inf
    )
    scores = jnp.dot(cmat, bmat.T, precision=HIGHEST_PREC)
    weights = jnp.exp(gap_decay) * scores[:, :, None] * step_size[None, :, :]
    block_out = jnp.einsum("tsh,shp->thp", weights, inner_x, precision=HIGHEST_PREC)
    enter = jnp.where((seg_ids == last_seg)[:, None], jnp.exp(cum_decay), 0.0)
    block_out = block_out + enter[:, :, None] * jnp.einsum(
        "tn,hpn->thp", cmat, state, precision=HIGHEST_PREC
    )
    tail_weight = (
        jnp.where(
            (seg_ids == seg_ids[-1])[:, None], jnp.exp(cum_decay[-1][None, :] - cum_decay), 0.0
        )
        * step_size
    )
    carry_keep = jnp.where(seg_ids[-1] == last_seg, jnp.exp(cum_decay[-1]), 0.0)
    new_state = carry_keep[:, None, None] * state + jnp.einsum(
        "sh,shp,sn->hpn", tail_weight, inner_x, bmat, precision=HIGHEST_PREC
    )
    return ((new_state, seg_ids[-1]), block_out)


def link_states(earlier, later):
    gain_a, state_a, first_a, last_a = earlier
    gain_b, state_b, first_b, last_b = later
    joined = (first_b == last_a) | (last_a < 0.0) | (first_b < 0.0)
    passing = jnp.where(joined, gain_b, 0.0)
    merged_gain = gain_a * passing
    merged_state = passing[:, None, None] * state_a + state_b
    merged_first = jnp.where(first_a < 0.0, first_b, first_a)
    merged_last = jnp.where(last_b < 0.0, last_a, last_b)
    return (merged_gain, merged_state, merged_first, merged_last)


def local(
    tokens, w_zx, w_bc, w_dt, dt_bias, a_rate, d_skip, conv_x, conv_bc, norm_gain, w_out, segments
):
    tok_rows = tokens.shape[0]
    inner_w = w_zx.shape[2]
    heads = dt_bias.shape[0]
    head_size = inner_w // heads
    state_w = w_bc.shape[1] // 2
    rim_len = conv_x.shape[0] - 1
    piece = lax.all_gather(tokens, "tensor", axis=1, tiled=True)
    gate_rows = w_zx[0]
    inner_rows = w_zx[1]
    gate_sum = jnp.dot(piece, gate_rows, preferred_element_type=jnp.float32)
    inner_sum = jnp.dot(piece, inner_rows, preferred_element_type=jnp.float32)
    bc_sum = jnp.dot(piece, w_bc, preferred_element_type=jnp.float32)
    dt_raw = jnp.dot(piece, w_dt, preferred_element_type=jnp.float32)
    gate_proj = gate_sum.astype(jnp.bfloat16)
    inner_proj = inner_sum.astype(jnp.bfloat16)
    bc_proj = bc_sum.astype(jnp.bfloat16)
    rim_inner, rim_bc, rim_seg = from_behind(
        (
            inner_proj[tok_rows - rim_len :],
            bc_proj[tok_rows - rim_len :],
            segments[tok_rows - rim_len :].astype(jnp.bfloat16),
        ),
        "seq",
        1,
    )
    seg_ext = jnp.concatenate([rim_seg.astype(jnp.int32), segments], 0)
    conv_inner = conv_tail(
        jnp.concatenate([rim_inner.astype(jnp.float32), inner_proj.astype(jnp.float32)], 0),
        seg_ext,
        conv_x,
        tok_rows,
    )
    conv_state = conv_tail(
        jnp.concatenate([rim_bc.astype(jnp.float32), bc_proj.astype(jnp.float32)], 0),
        seg_ext,
        conv_bc,
        tok_rows,
    )
    bmat = conv_state[:, :state_w]
    cmat = conv_state[:, state_w:]
    step_size = jax.nn.softplus(dt_raw + dt_bias)
    logdec = -a_rate * step_size
    inner_heads = conv_inner.reshape(tok_rows, heads, head_size)
    nblocks = tok_rows // BLOCK
    blocks = (
        inner_heads.reshape(nblocks, BLOCK, heads, head_size),
        step_size.reshape(nblocks, BLOCK, heads),
        logdec.reshape(nblocks, BLOCK, heads),
        bmat.reshape(nblocks, BLOCK, state_w),
        cmat.reshape(nblocks, BLOCK, state_w),
        segments.reshape(nblocks, BLOCK),
    )
    start_carry = (jnp.zeros((heads, head_size, state_w), jnp.float32), jnp.array(-1, jnp.int32))
    (local_state, _), block_outs = lax.scan(ssd_block, start_carry, blocks)
    cum_device = jnp.cumsum(logdec, axis=0)
    device_gain = jnp.where(segments[0] == segments[-1], jnp.exp(cum_device[-1]), 0.0)
    seg_float = segments.astype(jnp.float32)
    element = (device_gain, local_state, seg_float[:1], seg_float[-1:])
    identity = (
        jnp.ones((heads,), jnp.float32),
        jnp.zeros_like(local_state),
        jnp.full((1,), -1.0, jnp.float32),
        jnp.full((1,), -1.0, jnp.float32),
    )
    incoming = entering(element, "seq", link_states, identity)
    state_in = incoming[1]
    last_in = incoming[3]
    enter = jnp.where((seg_float == last_in[0])[:, None], jnp.exp(cum_device), 0.0)
    ssd_out = block_outs.reshape(tok_rows, heads, head_size)
    ssd_out = ssd_out + enter[:, :, None] * jnp.einsum(
        "tn,hpn->thp", cmat, state_in, precision=HIGHEST_PREC
    )
    ssd_out = ssd_out + d_skip[None, :, None] * inner_heads
    gated = ssd_out.reshape(tok_rows, inner_w) * jax.nn.silu(gate_proj.astype(jnp.float32))
    local_squares = jnp.sum(gated * gated, axis=1)
    total_squares = lax.psum(local_squares, "tensor")
    scale = lax.rsqrt(total_squares / (inner_w * lax.axis_size("tensor")) + NORM_EPS)
    normed = (gated * scale[:, None] * norm_gain).astype(jnp.bfloat16)
    return lax.psum_scatter(
        jnp.dot(normed, w_out, preferred_element_type=jnp.float32).astype(jnp.bfloat16),
        "tensor",
        scatter_dimension=0,
        tiled=True,
    )


def solution(mesh):
    in_specs = (
        P("seq", "tensor"),
        P(None, None, "tensor"),
        P(),
        P(None, "tensor"),
        P("tensor"),
        P("tensor"),
        P("tensor"),
        P(None, "tensor"),
        P(),
        P("tensor"),
        P("tensor", None),
        P("seq"),
    )
    out_specs = P(("seq", "tensor"), None)
    return jax.shard_map(local, mesh=mesh, in_specs=in_specs, out_specs=out_specs, check_vma=False)
```

profile of v0, /device:TPU:25, one launch (start us, length us, event | category | flops | bytes accessed | tf_op | source)
XLA Modules:
  0.0 465.7 jit_solution(9409055045789982205)
XLA Ops:
  6.5 0.7 all-gather.6.cloned.1.call-update
  7.3 0.8 convert_convert_fusion
  8.2 1.3 dynamic-slice
  10.0 1.4 dynamic-update-slice
  11.4 1.3 dynamic-update-slice.1
  12.7 1.3 collective-permute-start
  14.0 11.9 %all-reduce.2 = (bf16[8]{0:T(256)(128)(2,1)S(1)}, bf16[8]{0:T(256)(128)(2,1)S(1)}) all-reduce(bf16[8]{0:T(256)(128)(2,1)S(1)} %dynamic-update-slice, bf16[8]{0:T(256)(128)(2,1)S(1)} %dynamic-update-slice.1), channel_id=2, replica_groups=mesh['seq'=8,'tensor'=32] {'seq'}, use_global_device_ids=true, to_apply=%add | all-reduce | flops 16 | bytes 64
  25.9 0.7 reshape.139
  26.6 0.7 neg.20
  27.2 1.4 fusion.81
  29.9 0.8 slice_bitcast_fusion.8
  30.8 0.8 slice_bitcast_fusion.4
  31.6 0.8 pad_add_fusion
  32.4 0.8 slice_compare_fusion.2
  33.1 56.2 %all-gather.6.cloned.1.call-done = bf16[512,3584]{0,1:T(8,128)(2,1)} async-done(((bf16[512,112]{0,1:T(8,128)(2,1)}), bf16[512,3584]{0,1:T(8,128)(2,1)}) %all-gather.6.cloned.1.call-update) | async-done | bytes 3670032 | tf_op jit(solution)/shard_map/all_gather | solution.py:104
  89.4 2.7 broadcast_multiply_fusion
  92.2 3.6 fusion.83
  95.8 1.3 collective-permute-start.1
  97.1 1.1 fusion.84
  98.3 1.3 collective-permute-start.2
  100.9 14.4 %all-gather.3 = bf16[8,1,2]{2,1,0:T(2,128)(2,1)S(1)} all-gather(bf16[1,1,2]{2,1,0:T(2,128)(2,1)S(1)} %bitcast.197), channel_id=1, replica_groups=mesh['seq'=8,'tensor'=32] {'seq'}, dimensions={0}, use_global_device_ids=true | all-gather | bytes 36 | tf_op jit(solution)/shard_map/all_gather | solution.py:22
  117.0 16.2 %while.31 = (s32[]{:T(128)}, f32[2,64,64]{2,1,0:T(8,128)S(1)}, s32[]{:T(128)}, f32[2,256,2,64]{1,0,3,2:T(2,128)S(1)}, s32[2,256]{1,0:T(2,128)S(1)}, /*index=5*/f...) while((s32[]{:T(128)}, f32[2,64,64]{2,1,0:T(8,128)S(1)}, ...), condition=%wide.region_3.4_spmd.clone, body=%wide.region_0.3_spmd.clone.sunk | while | flops 202246672 | bytes 2326889 | solution.py:151
  121.7 0.8 fusion.114
  122.6 1.9 dynamic_update_slice.6
  129.8 0.8 fusion.114
  130.7 1.9 dynamic_update_slice.6
  133.4 12.8 %all-gather.1 = bf16[16,64,64]{2,1,0:T(8,128)(2,1)S(1)} all-gather(bf16[2,64,64]{2,1,0:T(8,128)(2,1)S(1)} %convert_element_type.85), channel_id=3, replica_groups=mesh['seq'=8,'tensor'=32] {'seq'}, dimensions={0}, use_global_device_ids=true | all-gather | bytes 147456 | tf_op jit(solution)/shard_map/all_gather | solution.py:22
  146.3 24.2 %while.30 = (s32[]{:T(128)}, f32[2,64,64]{2,1,0:T(8,128)S(1)}, f32[1]{0:T(128)}, s32[]{:T(128)}, bf16[8,1]{0,1:T(2,128)(2,1)S(1)}, /*index=5*/bf16[8,2]{0,1:T(2,...) while((s32[]{:T(128)}, f32[2,64,64]{2,1,0:T(8,128)S(1)}, ...), condition=%wide.region_7.8_spmd, body=%wide.region_6.7_spmd.sunk | while | flops 24592 | bytes 82183 | solution.py:38
  171.2 3.5 multiply_reduce_fusion
  174.7 58.0 %psum.7 = f32[512]{0:T(512)S(1)} all-reduce(f32[512]{0:T(512)S(1)} %get-tuple-element.290), channel_id=1, replica_groups=mesh['seq'=8,'tensor'=32] {'tensor'}, use_global_device_ids=true, to_apply=%region_9.10 | all-reduce | flops 512 | bytes 4096 | tf_op jit(solution)/shard_map/psum | solution.py:173
  232.7 3.0 convolution_convert_fusion
  235.7 223.2 %reduce-scatter.2.cloned.1.call-done = bf16[16,3584]{1,0:T(8,128)(2,1)} async-done(((bf16[512,3584]{1,0:T(8,128)(2,1)}), bf16[16,3584]{1,0:T(8,128)(2,1)}) %reduce-scatter.2.cloned.1.call-update) | async-done | bytes 114704 | tf_op jit(solution)/shard_map/reduce_scatter | solution.py:176
  (134 shorter events, 19.1 us)
Async XLA Ops:
  6.5 226.1 %copy-start = (bf16[128,3584]{1,0:T(8,128)(2,1)S(1)}, bf16[128,3584]{1,0:T(8,128)(2,1)}, u32[]{:S(2)}) copy-start(bf16[128,3584]{1,0:T(8,128)(2,1)} %param.26) | copy-start | bytes 2752516
  6.5 82.8 %all-gather.6.cloned.1.call-start = ((), (), s32[]{:S(2)}) async-start(), calls=%async_computation.1 | async-start | bytes 3784704 | tf_op jit(solution)/shard_map/all_gather | solution.py:104
  7.3 451.6 %reduce-scatter.2.cloned.1.call-start = ((), (), s32[]{:S(2)}) async-start(), calls=%async_computation.2 | async-start | bytes 3784704 | tf_op jit(solution)/shard_map/reduce_scatter | solution.py:176
  12.7 18.9 %collective-permute-start = (bf16[3]{0:T(256)(128)(2,1)S(1)}, bf16[3]{0:T(256)(128)(2,1)S(1)}, u32[]{:S(2)}, u32[]{:S(2)}) collective-permute-start(bf16[3]{0:T(256)(128)(2,1)S(1)} %slice.118), channel_id=1, source_target_pairs={{0,32},{32,64},{64,96},{96,128},{128,160},{160,192},{192,224},{1,3... | collective-permute-start | bytes 26 | tf_op jit(solution)/shard_map/ppermute | solution.py:16
  92.0 5.1 %copy-start.2 = (bf16[3584,128]{1,0:T(8,128)(2,1)S(1)}, bf16[3584,128]{1,0:T(8,128)(2,1)}, u32[]{:S(2)}) copy-start(bf16[3584,128]{1,0:T(8,128)(2,1)} %param.18) | copy-start | bytes 2752516
  92.2 4.9 %copy-start.1 = (bf16[512,3584]{0,1:T(8,128)(2,1)S(1)}, bf16[512,3584]{0,1:T(8,128)(2,1)}, u32[]{:S(2)}) copy-start(bf16[512,3584]{0,1:T(8,128)(2,1)} %all-gather.6.cloned.1.call-done) | copy-start | bytes 11010052
  95.8 19.5 %collective-permute-start.1 = (bf16[3,128]{1,0:T(4,128)(2,1)S(1)}, bf16[3,128]{1,0:T(4,128)(2,1)S(1)}, u32[]{:S(2)}, u32[]{:S(2)}) collective-permute-start(bf16[3,128]{1,0:T(4,128)(2,1)S(1)} %slice.152), channel_id=1, source_target_pairs={{0,32},{32,64},{64,96},{96,128},{128,160},{160,192},{192,224},{1,3... | collective-permute-start | bytes 2312 | tf_op jit(solution)/shard_map/ppermute | solution.py:16
  98.3 18.0 %collective-permute-start.2 = (bf16[3,128]{1,0:T(4,128)(2,1)S(1)}, bf16[3,128]{1,0:T(4,128)(2,1)S(1)}, u32[]{:S(2)}, u32[]{:S(2)}) collective-permute-start(bf16[3,128]{1,0:T(4,128)(2,1)S(1)} %slice.157), channel_id=1, source_target_pairs={{0,32},{32,64},{64,96},{96,128},{128,160},{160,192},{192,224},{1,3... | collective-permute-start | bytes 2312 | tf_op jit(solution)/shard_map/ppermute | solution.py:16
  117.0 53.4 %copy-start.3 = (s32[512]{0:T(512)S(1)}, s32[512]{0:T(512)}, u32[]{:S(2)}) copy-start(s32[512]{0:T(512)} %param.27) | copy-start | bytes 6148
  117.0 53.5 %copy-start.5 = (f32[2]{0:T(128)S(1)}, f32[2]{0:T(128)}, u32[]{:S(2)}) copy-start(f32[2]{0:T(128)} %param.22) | copy-start | bytes 28
  171.0 61.7 %copy-start.4 = (f32[128]{0:T(128)S(1)}, f32[128]{0:T(128)}, u32[]{:S(2)}) copy-start(f32[128]{0:T(128)} %param.25) | copy-start | bytes 1540
Sparse Core Ops, SparseCore 0:
  9.9 79.3 all-gather.5
  235.8 223.0 reduce-scatter.1
where the time goes:
time: 472 us; the launch traced here: 466 us
  waiting for transfers between devices  280 us (59%)
  blocking collectives  97.1 us (21%)
  local copies, waits for them, and re-layouts  22.1 us (5%)
  loops' own time  20.8 us (4%)
  matrix products  17.9 us (4%)
  between operations  15 us (3%)
  other arithmetic  8.78 us (2%)
    reduce_scatter x1, waiting for transfers between devices, local(): lax.psum_scatter(jnp.dot(normed, w_out, preferred_element_type=jnp.float3...  223 us
    psum x1, blocking collectives, local(): total_squares = lax.psum(local_squares, 'tensor')  58 us
    all_gather x1, waiting for transfers between devices, local(): piece = lax.all_gather(tokens, 'tensor', axis=1, tiled=True)  56.2 us
    all_gather x2, blocking collectives, entering(): lax.all_gather(a.astype(kind), axis)  27.2 us
    another operation x1, loops' own time, entering(): return lax.fori_loop(0, place, one, state)  18.1 us
    unnamed x1, blocking collectives  11.9 us
  transfers between devices with their start and end apart: 5, of which 2 were waited for; matrix products, arithmetic and copies ran while one was open for 3% of the time, Pallas kernels for 0%

commit v1 on v0

v1 whole, which is shorter than its diff:
```python
import jax
import jax.numpy as jnp
from jax import lax
from jax.experimental import pallas as pl
from jax.experimental.pallas import tpu as pltpu
from jax.sharding import PartitionSpec as P

NORM_EPS = 1e-05
TOK = 512
FEAT = 112
DEPTH = 3584
QUART = DEPTH // 4
WIDE = DEPTH + 128
HALF = 256
MESH = pl.DeviceIdType.MESH
F32 = jnp.float32
BF16 = jnp.bfloat16


def silu(v):
    return v / (1.0 + jnp.exp(-v))


def softplus(v):
    return jnp.maximum(v, 0.0) + jnp.log1p(jnp.exp(-jnp.abs(v)))


def dot_tn(a, b):
    return lax.dot_general(a, b, (((0,), (0,)), ((), ())), preferred_element_type=F32)


def dot_nt(a, b):
    return lax.dot_general(a, b, (((1,), (1,)), ((), ())), preferred_element_type=F32)


def dot_nn(a, b):
    return jnp.dot(a, b, preferred_element_type=F32)


def three_parts(v):
    hi = v.astype(BF16)
    rest = v - hi.astype(F32)
    mid = rest.astype(BF16)
    low = (rest - mid.astype(F32)).astype(BF16)
    return hi, mid, low


def kernel(
    tok_hbm, wzx_hbm, wbc_hbm, wdt_hbm, small_hbm, tapbc_ref, wout_hbm, seg_hbm,
    out_ref,
    G, WZ, WB, WD, SM, SEG, WO, ACC, LT, HXS, HXR, STS, STR, GN, PS,
    RXF, RXC, RXS, RZF, RZC, RZS, FS, FR,
    SS, RG, RW, RO, RM, RH, RS, RN, RF, RC, RX, RZ, LC,
):
    seq, ten = lax.axis_index("seq"), lax.axis_index("tensor")
    y, c = seq // 2, seq % 2
    z, x = ten // 4, ten % 4
    w, kap = z // 2, z % 2
    blk = 2 * y + kap
    sgn = 1 - 2 * c
    native = c == kap
    foreign = c != kap

    def m4(v):
        return (v + 8) % 4

    def dev(yy, zz, xx, cc):
        return (2 * yy + cc, 4 * zz + xx)

    core = dev(y, z, x, 1 - c)

    def dx(k):
        return dev(y, z, m4(x + k), c)

    def dw(k):
        return dev(y, 2 * m4(w + k) + kap, x, c)

    def dy(k):
        return dev(m4(y + k), z, x, c)

    other_z = z + 1 - 2 * kap
    swap = dev(y, other_z, x, 1 - c)
    twin = dev(y, other_z, x, c)

    def chain(b):
        return dev(b // 2, 2 * w + b % 2, x, c)

    count = [0]
    pending = []

    def send(src, dst, rsem, device, track=True):
        k = count[0]
        count[0] += 1
        cp = pltpu.make_async_remote_copy(
            src_ref=src, dst_ref=dst, send_sem=SS.at[k], recv_sem=rsem,
            device_id=device, device_id_type=MESH,
        )
        cp.start()
        if track:
            pending.append(cp)
        return cp

    def arrive(dst, rsem):
        pltpu.make_async_remote_copy(
            src_ref=dst, dst_ref=dst, send_sem=SS.at[0], recv_sem=rsem,
            device_id=core, device_id_type=MESH,
        ).wait_recv()

    def gslot(f):
        return G.at[pl.ds(pl.multiple_of(f * FEAT, 16), FEAT), :]

    def fid(wj, xj, cc):
        return 8 * m4(wj) + 4 * cc + m4(xj)

    def gsend(wj, xj, device):
        f = fid(wj, xj, c)
        send(gslot(f), gslot(f), RG.at[f], device)

    def gwait(wj, xj, cc):
        f = fid(wj, xj, cc)
        arrive(gslot(f), RG.at[f])

    def orow(par):
        return pl.ds(pl.multiple_of(128 * par, 128), 128)

    own_f = fid(w, x, c)
    l_wb = pltpu.make_async_copy(wbc_hbm, WB, LC.at[0])
    l_wo = pltpu.make_async_copy(wout_hbm, WO.at[orow(kap), :], LC.at[1])
    l_tok = pltpu.make_async_copy(tok_hbm, gslot(own_f), LC.at[2])
    l_wz = pltpu.make_async_copy(wzx_hbm, WZ, LC.at[3])
    l_wd = pltpu.make_async_copy(wdt_hbm, WD, LC.at[4])
    l_sm = pltpu.make_async_copy(small_hbm, SM, LC.at[5])
    l_sg = pltpu.make_async_copy(seg_hbm, SEG, LC.at[6])

    @pl.when(native)
    def _():
        l_tok.start()
        l_sg.start()
        l_wz.start()
        l_wd.start()
        l_sm.start()

    l_wb.start()
    l_wo.start()

    barrier = pltpu.get_barrier_semaphore()
    peers = [core, dx(1), dx(3), dw(1), dw(3), swap]
    peers += [chain((blk + k) % 8) for k in range(1, 8)]
    for p in peers:
        pl.semaphore_signal(barrier, inc=1, device_id=p, device_id_type=MESH)
    rows = lax.broadcasted_iota(jnp.int32, (TOK, TOK), 0)
    cols = lax.broadcasted_iota(jnp.int32, (TOK, TOK), 1)
    LT[...] = jnp.where(rows <= cols, 1.0, 0.0).astype(BF16)
    pl.semaphore_wait(barrier, len(peers))

    quart = pl.ds(pl.multiple_of(y * QUART, 128), QUART)

    def qrow(k):
        return pl.ds(pl.multiple_of(m4(y + k) * QUART, 128), QUART)

    k0 = count[0]
    count[0] += 4

    def sp_send(k, src, dst, rsem, device):
        return pltpu.make_async_remote_copy(
            src_ref=src, dst_ref=dst, send_sem=SS.at[k0 + k], recv_sem=rsem,
            device_id=device, device_id_type=MESH,
        )

    f_swap = fid(w, x, 1 - c)
    s_swap = sp_send(0, tok_hbm, gslot(f_swap), RG.at[f_swap], swap)
    s_seg = sp_send(0, seg_hbm, SEG, RM.at[2], core)
    s_wz = sp_send(1, wzx_hbm.at[:, quart, :], WZ.at[:, quart, :], RW.at[0], twin)
    s_wd = sp_send(2, wdt_hbm, WD, RM.at[0], twin)
    s_sm = sp_send(3, small_hbm, SM, RM.at[1], twin)

    @pl.when(foreign)
    def _():
        s_swap.start()
        gwait(w, x, c)

    @pl.when(native)
    def _():
        s_seg.start()
        l_tok.wait()

    gsend(w, x, dw(1))
    gsend(w, x, dw(3))
    gsend(w, x, dx(1))
    gsend(w, x, dx(3))
    gsend(w, x, core)

    @pl.when(native)
    def _():
        s_wd.start()
        s_sm.start()
        s_wz.start()

    def pass_x(wj):
        gwait(wj, x - sgn, c)
        gsend(wj, x - sgn, dx(sgn))
        gsend(wj, x - sgn, core)

    def spread_x(wj):
        gsend(wj, x, dx(1))
        gsend(wj, x, dx(3))
        gsend(wj, x, core)

    def to_core(wj, xj):
        gwait(wj, xj, c)
        gsend(wj, xj, core)

    pass_x(w)
    gwait(w - sgn, x, c)
    gsend(w - sgn, x, dw(sgn))
    spread_x(w - sgn)
    gwait(w + sgn, x, c)
    spread_x(w + sgn)
    to_core(w, x + sgn)

    kw = count[0]
    count[0] += 10

    def wsend(k, src, dst, rsem, device):
        return pltpu.make_async_remote_copy(
            src_ref=src, dst_ref=dst, send_sem=SS.at[kw + k], recv_sem=rsem,
            device_id=device, device_id_type=MESH,
        )

    def wz_at(k):
        return WZ.at[:, qrow(k), :]

    w_up = wsend(0, wz_at(0), wz_at(0), RW.at[1], dy(1))
    w_down = wsend(1, wz_at(0), wz_at(0), RW.at[2], dy(3))
    w_fg = wsend(2, WZ.at[0, qrow(-1), :], WZ.at[0, qrow(-1), :], RW.at[3], dy(1))
    w_fi = wsend(3, WZ.at[1, qrow(1), :], WZ.at[1, qrow(1), :], RW.at[4], dy(3))
    other = orow(1 - kap)

    def wo_at(k, lo=0, n=128):
        return WO.at[pl.ds(pl.multiple_of(128 * (1 - kap) + lo, 64), n), qrow(k)]

    o_first = wsend(
        4, wout_hbm.at[:, quart], WO.at[orow(kap), quart], RO.at[0], twin
    )
    o_up = wsend(4, wo_at(0), wo_at(0), RO.at[1], dy(1))
    o_down = wsend(5, wo_at(0), wo_at(0), RO.at[2], dy(3))
    o_fg = wsend(6, wo_at(-1, 0, 64), wo_at(-1, 0, 64), RO.at[3], dy(1))
    o_fi = wsend(7, wo_at(1, 64, 64), wo_at(1, 64, 64), RO.at[4], dy(3))
    o_core = wsend(8, WO.at[other, :], WO.at[other, :], RO.at[5], core)

    @pl.when(foreign)
    def _():
        arrive(wz_at(0), RW.at[0])
        w_up.start()
        w_down.start()

    pass_x(w - sgn)
    pass_x(w + sgn)
    gwait(w + 2, x, c)
    spread_x(w + 2)

    @pl.when(native)
    def _():
        o_first.start()

    to_core(w, x + 2)
    to_core(w - sgn, x + sgn)
    to_core(w + sgn, x + sgn)
    pass_x(w + 2)

    @pl.when(foreign)
    def _():
        arrive(wz_at(-1), RW.at[1])
        w_fg.start()
        arrive(wz_at(1), RW.at[2])
        w_fi.start()
        arrive(wo_at(0), RO.at[0])
        o_up.start()
        o_down.start()

    to_core(w - sgn, x + 2)
    to_core(w + sgn, x + 2)
    to_core(w + 2, x + sgn)
    to_core(w + 2, x + 2)

    @pl.when(foreign)
    def _():
        arrive(WZ.at[0, qrow(2), :], RW.at[3])
        arrive(WZ.at[1, qrow(2), :], RW.at[4])
        arrive(WD, RM.at[0])
        arrive(SM, RM.at[1])
        arrive(SEG, RM.at[2])

    @pl.when(native)
    def _():
        l_wz.wait()
        l_wd.wait()
        l_sm.wait()
        l_sg.wait()

    l_wb.wait()

    for i, wj in enumerate((w, w - sgn, w + sgn, w + 2)):
        for xj in range(4):
            gwait(wj, xj, 1 - c)
        krow = pl.ds(pl.multiple_of(m4(wj) * QUART, 128), QUART)
        gk = G[krow, :]
        parts = (
            dot_tn(WZ[0, krow, :], gk),
            dot_tn(WZ[1, krow, :], gk),
            dot_tn(WB[krow, :], gk),
        )
        for j, part in enumerate(parts):
            at = slice(128 * j, 128 * j + 128)
            ACC[at, :] = part if i == 0 else ACC[at, :] + part

    dt_raw = dot_nn(WD[...], G[...])

    @pl.when(foreign)
    def _():
        arrive(wo_at(-1), RO.at[1])
        o_fg.start()
        arrive(wo_at(1), RO.at[2])
        o_fi.start()

    seg = SEG[...].astype(F32)
    HXS[0:256, :] = ACC[128:384, TOK - 128:].astype(BF16)
    HXS[256:272, :] = jnp.broadcast_to(seg[:, TOK - 128:], (16, 128)).astype(BF16)
    kh = count[0]
    count[0] += 8
    h_send = pltpu.make_async_remote_copy(
        src_ref=HXS, dst_ref=HXR, send_sem=SS.at[kh], recv_sem=RH.at[0],
        device_id=chain((blk + 1) % 8), device_id_type=MESH,
    )

    @pl.when(blk < 7)
    def _():
        h_send.start()

    @pl.when(blk == 0)
    def _():
        HXR[0:256, :] = jnp.zeros((256, 128), BF16)
        HXR[256:272, :] = jnp.full((16, 128), -1.0, BF16)

    sm = SM[...]
    smt = jnp.concatenate([sm, jnp.zeros((120, 128), F32)], 0).T
    step = softplus(dt_raw + smt[0:2, 6:7])
    logdec = -smt[0:2, 7:8] * step
    hi, mid, low = three_parts(logdec)
    pieces = jnp.concatenate(
        [hi.astype(F32), mid.astype(F32), low.astype(F32), jnp.zeros((2, TOK), F32)], 0
    ).astype(BF16)
    sums = dot_nn(pieces, LT[...])
    cum = sums[0:2] + sums[2:4] + sums[4:6]
    total = cum[:, TOK - 1:]
    last_seg = seg[:, TOK - 1:]
    first_seg = seg[:, 0:1]
    tail = jnp.where(seg == last_seg, jnp.exp(total - cum), 0.0)
    enter = jnp.where(seg == first_seg, jnp.exp(cum), 0.0)
    colmat = jnp.concatenate([cum, seg, jnp.zeros((125, TOK), F32)], 0).T

    tb = jnp.concatenate([tapbc_ref[...], jnp.zeros((120, 128), F32)], 0).T

    def conv(before, now, seg_before, seg_now, taps):
        both = jnp.concatenate([before, now], 1)
        seg_both = jnp.broadcast_to(
            jnp.concatenate([seg_before, seg_now], 1), (8, both.shape[1])
        )
        total_sum = taps[:, 3:4] * now
        for off in (1, 2, 3):
            same = pltpu.roll(seg_both, off, 1)[0:1, 128:] == seg_now
            moved = pltpu.roll(both, off, 1)[:, 128:]
            total_sum = total_sum + taps[:, 3 - off:4 - off] * jnp.where(same, moved, 0.0)
        return silu(total_sum)

    def rounded(v):
        return v.astype(BF16).astype(F32)

    @pl.when(blk > 0)
    def _():
        arrive(HXR, RH.at[0])

    halo = HXR[...].astype(F32)
    seg_halo = halo[256:257, :]
    xin = conv(halo[0:128], rounded(ACC[128:256, :]), seg_halo, seg, smt)
    bcin = conv(halo[128:256], rounded(ACC[256:384, :]), seg_halo, seg, tb)
    bt = bcin[0:64].astype(BF16)
    ct = bcin[64:128].astype(BF16)

    def by_head(v):
        return jnp.concatenate(
            [jnp.broadcast_to(v[0:1], (64, TOK)), jnp.broadcast_to(v[1:2], (64, TOK))], 0
        )

    xdt = xin * by_head(step)
    state = dot_nt(bt, (xdt * by_head(tail)).astype(BF16))
    lane = lax.broadcasted_iota(jnp.int32, (1, 128), 1)
    tot_lane = jnp.where(lane < 64, total[0:1], total[1:2])
    hi, mid, low = three_parts(tot_lane)
    STS[0:64, :] = state.astype(BF16)
    STS[64:80, :] = jnp.concatenate(
        [hi.astype(F32), mid.astype(F32), low.astype(F32),
         jnp.broadcast_to(last_seg, (13, 128))], 0
    ).astype(BF16)
    st_sends = []
    for k in range(1, 8):
        st_sends.append(
            pltpu.make_async_remote_copy(
                src_ref=STS, dst_ref=STR.at[k - 1], send_sem=SS.at[kh + k],
                recv_sem=RS.at[k - 1], device_id=chain((blk + k) % 8), device_id_type=MESH,
            )
        )

        @pl.when(blk + k < 8)
        def _(k=k):
            st_sends[k - 1].start()

    xb = xdt.astype(BF16)
    yacc = [[None, None], [None, None]]
    for si, ti in ((0, 0), (0, 1), (1, 1)):
        ss, ts = slice(256 * si, 256 * si + 256), slice(256 * ti, 256 * ti + 256)
        scores = dot_tn(bt[:, ss], ct[:, ts])
        seen = colmat[ss, 2:3] == seg[:, ts]
        if si == ti:
            seen = seen & (
                lax.broadcasted_iota(jnp.int32, (256, 256), 0)
                <= lax.broadcasted_iota(jnp.int32, (256, 256), 1)
            )
        for h in (0, 1):
            gap = jnp.where(seen, cum[h:h + 1, ts] - colmat[ss, h:h + 1], -jnp.inf)
            mat = (jnp.exp(gap) * scores).astype(BF16)
            part = dot_nn(xb[64 * h:64 * h + 64, ss], mat)
            yacc[ti][h] = part if yacc[ti][h] is None else yacc[ti][h] + part
    inner = jnp.concatenate(
        [jnp.concatenate(yacc[0], 0), jnp.concatenate(yacc[1], 0)], 1
    )
    ACC[128:256, :] = inner + smt[:, 5:6] * xin

    ACC[256:320, 0:128] = jnp.zeros((64, 128), F32)
    ACC[320:328, 0:128] = jnp.zeros((8, 128), F32)
    for k in range(1, 8):
        @pl.when(blk >= k)
        def _(k=k):
            arrive(STR.at[k - 1], RS.at[k - 1])
            got = STR[k - 1].astype(F32)
            run = ACC[320:321, 0:128]
            weight = jnp.where(got[67:68] == first_seg, jnp.exp(run), 0.0)
            ACC[256:320, 0:128] += weight * got[0:64]
            ACC[320:321, 0:128] = run + (got[64:65] + got[65:66] + got[66:67])

    state_in = ACC[256:320, 0:128].astype(BF16)
    yout = ACC[128:256, :] + dot_tn(state_in, ct) * by_head(enter)
    gated = yout * silu(rounded(ACC[0:128, :]))
    scaled = gated * smt[:, 4:5]
    squares = gated * gated
    for j in range(4):
        js = slice(128 * j, 128 * j + 128)
        gj = scaled[:, js].T.astype(BF16)
        qj = squares[:, js].T.astype(BF16)
        for par in (0, 1):
            ps = slice(64 * par, 64 * par + 64)
            GN[c, j, par, :, 0:128] = gj[ps]
            GN[c, j, par, :, 128:256] = qj[ps]
    send(GN.at[c, :, 1 - c], GN.at[c, :, 1 - c], RN.at[0], core)

    @pl.when(foreign)
    def _():
        arrive(wo_at(2, 0, 64), RO.at[3])
        arrive(wo_at(2, 64, 64), RO.at[4])
        o_core.start()

    l_wo.wait()

    @pl.when(native)
    def _():
        arrive(WO.at[other, :], RO.at[5])

    arrive(GN.at[1 - c, :, c], RN.at[0])

    def product(wj):
        j = m4(wj)
        a = GN[0, j, c]
        b = GN[1, j, c]
        lhs = jnp.concatenate([a[:, 0:128], b[:, 0:128]], 1)
        for n in range(7):
            ns = slice(512 * n, 512 * n + 512)
            res = dot_nn(lhs, WO[:, ns]).astype(BF16)
            for r in range(4):
                PS[j, r, :, ns] = res[16 * r:16 * r + 16]
        sq = (a[:, 128:256].astype(F32) + b[:, 128:256].astype(F32)).astype(BF16)
        for r in range(4):
            PS[j, r, :, DEPTH:] = sq[16 * r:16 * r + 16]

    def chunk(wj, xj):
        return PS.at[m4(wj), m4(xj)]

    def outward(wj):
        j = m4(wj)
        product(wj)
        send(chunk(wj, x + 2), RXF.at[j], RX.at[0, j], dx(sgn))
        send(chunk(wj, x - sgn), RXS.at[j], RX.at[2, j], dx(-sgn))

    def combine(wj):
        j = m4(wj)
        arrive(RXF.at[j], RX.at[0, j])
        r = m4(x + sgn)
        PS[j, r] = (PS[j, r].astype(F32) + RXF[j].astype(F32)).astype(BF16)
        send(chunk(wj, x + sgn), RXC.at[j], RX.at[1, j], dx(sgn))

    def summed(wj):
        j = m4(wj)
        arrive(RXC.at[j], RX.at[1, j])
        arrive(RXS.at[j], RX.at[2, j])
        return PS[j, x].astype(F32) + RXC[j].astype(F32) + RXS[j].astype(F32)

    outward(w + 2)
    outward(w + sgn)
    combine(w + 2)
    outward(w - sgn)
    combine(w + sgn)
    outward(w)
    combine(w - sgn)
    PS[m4(w + 2), x] = summed(w + 2).astype(BF16)
    send(chunk(w + 2, x), RZF, RZ.at[0], dw(sgn))
    combine(w)
    part = summed(w + sgn)
    arrive(RZF, RZ.at[0])
    PS[m4(w + sgn), x] = (part + RZF[...].astype(F32)).astype(BF16)
    send(chunk(w + sgn, x), RZC, RZ.at[1], dw(sgn))
    PS[m4(w - sgn), x] = summed(w - sgn).astype(BF16)
    send(chunk(w - sgn, x), RZS, RZ.at[2], dw(-sgn))
    part = summed(w)
    arrive(RZC, RZ.at[1])
    arrive(RZS, RZ.at[2])
    full = part + RZC[...].astype(F32) + RZS[...].astype(F32)
    mean = jnp.sum(full[:, DEPTH:], axis=1, keepdims=True) / 4096.0
    result = (full[:, 0:DEPTH] * lax.rsqrt(mean + NORM_EPS)).astype(BF16)
    kf = count[0]
    count[0] += 1
    f_send = pltpu.make_async_remote_copy(
        src_ref=FS, dst_ref=FR, send_sem=SS.at[kf], recv_sem=RF.at[0],
        device_id=swap, device_id_type=MESH,
    )

    @pl.when(foreign)
    def _():
        FS[...] = result
        f_send.start()

    @pl.when(native)
    def _():
        out_ref[...] = result

    for cp in pending:
        cp.wait_send()

    @pl.when(native)
    def _():
        s_seg.wait_send()
        s_wz.wait_send()
        s_wd.wait_send()
        s_sm.wait_send()
        o_first.wait_send()

    @pl.when(foreign)
    def _():
        s_swap.wait_send()
        for cp in (w_up, w_down, w_fg, w_fi, o_up, o_down, o_fg, o_fi, o_core):
            cp.wait_send()
        arrive(FR, RF.at[0])
        out_ref[...] = FR[...]
        f_send.wait_send()

    @pl.when(blk < 7)
    def _():
        h_send.wait_send()

    for k in range(1, 8):
        @pl.when(blk + k < 8)
        def _(k=k):
            st_sends[k - 1].wait_send()


def local(
    tokens, w_zx, w_bc, w_dt, dt_bias, a_rate, d_skip, conv_x, conv_bc, norm_gain, w_out, segments
):
    def wide(v):
        return jnp.pad(v, (0, 126))[None]

    small = jnp.concatenate(
        [conv_x, norm_gain[None], jnp.repeat(d_skip, 64)[None], wide(dt_bias), wide(a_rate)], 0
    )
    tapbc = jnp.pad(conv_bc, ((0, 4), (0, 0)))
    anywhere = pl.BlockSpec(memory_space=pl.ANY)
    inside = pl.BlockSpec(memory_space=pltpu.VMEM)
    dma = pltpu.SemaphoreType.DMA
    return pl.pallas_call(
        kernel,
        out_shape=jax.ShapeDtypeStruct((16, DEPTH), BF16),
        in_specs=[anywhere] * 5 + [inside] + [anywhere] * 2,
        out_specs=inside,
        scratch_shapes=[
            pltpu.VMEM((DEPTH, TOK), BF16),
            pltpu.VMEM((2, DEPTH, 128), BF16),
            pltpu.VMEM((DEPTH, 128), BF16),
            pltpu.VMEM((2, DEPTH), BF16),
            pltpu.VMEM((8, 128), F32),
            pltpu.VMEM((1, TOK), jnp.int32),
            pltpu.VMEM((256, DEPTH), BF16),
            pltpu.VMEM((384, TOK), F32),
            pltpu.VMEM((TOK, TOK), BF16),
            pltpu.VMEM((272, 128), BF16),
            pltpu.VMEM((272, 128), BF16),
            pltpu.VMEM((80, 128), BF16),
            pltpu.VMEM((7, 80, 128), BF16),
            pltpu.VMEM((2, 4, 2, 64, 256), BF16),
            pltpu.VMEM((4, 4, 16, WIDE), BF16),
            pltpu.VMEM((4, 16, WIDE), BF16),
            pltpu.VMEM((4, 16, WIDE), BF16),
            pltpu.VMEM((4, 16, WIDE), BF16),
            pltpu.VMEM((16, WIDE), BF16),
            pltpu.VMEM((16, WIDE), BF16),
            pltpu.VMEM((16, WIDE), BF16),
            pltpu.VMEM((16, DEPTH), BF16),
            pltpu.VMEM((16, DEPTH), BF16),
            dma((96,)),
            dma((32,)),
            dma((5,)),
            dma((6,)),
            dma((3,)),
            dma((1,)),
            dma((7,)),
            dma((1,)),
            dma((1,)),
            dma((1,)),
            dma((3, 4)),
            dma((3,)),
            dma((7,)),
        ],
        compiler_params=pltpu.CompilerParams(
            collective_id=0, has_side_effects=True, vmem_limit_bytes=48 * 1024 * 1024
        ),
        cost_estimate=pl.CostEstimate(
            flops=2 * TOK * DEPTH * 512, bytes_accessed=10_000_000, transcendentals=500_000
        ),
    )(tokens.T, w_zx, w_bc, w_dt.T, small, tapbc, w_out, segments.reshape(1, TOK))


def solution(mesh):
    in_specs = (
        P("seq", "tensor"),
        P(None, None, "tensor"),
        P(),
        P(None, "tensor"),
        P("tensor"),
        P("tensor"),
        P("tensor"),
        P(None, "tensor"),
        P(),
        P("tensor"),
        P("tensor", None),
        P("seq"),
    )
    out_specs = P(("seq", "tensor"), None)
    return jax.shard_map(local, mesh=mesh, in_specs=in_specs, out_specs=out_specs, check_vma=False)
```

time: 472 us -> 87.4 us (0.19); the launches traced: 466 us -> 86.9 us
  waiting for transfers between devices: 280 us -> 0 us
  blocking collectives: 97.1 us -> 0 us
  Pallas kernels: 0 us -> 77.3 us
  loops' own time: 20.8 us -> 0 us
  matrix products: 17.9 us -> 0 us
  between operations: 15 us -> 0.02 us
  local copies, waits for them, and re-layouts: 22.1 us -> 9.66 us
  other arithmetic: 8.78 us -> 0 us
    reduce_scatter x1 -> x0, waiting for transfers between devices: 223 us -> none  [local(): lax.psum_scatter(jnp.dot(normed, w_out, preferred_element_type=jnp.float3...]
    pallas_call x0 -> x1, Pallas kernels: none -> 77.3 us  [local(): pl.pallas_call(kernel, out_shape=jax.ShapeDtypeStruct((16, DEPTH), BF16),...]
    psum x1 -> x0, blocking collectives: 58 us -> none  [local(): total_squares = lax.psum(local_squares, 'tensor')]
    all_gather x1 -> x0, waiting for transfers between devices: 56.2 us -> none  [local(): piece = lax.all_gather(tokens, 'tensor', axis=1, tiled=True)]
    all_gather x2 -> x0, blocking collectives: 27.2 us -> none  [entering(): lax.all_gather(a.astype(kind), axis)]
    another operation x2 -> x0, loops' own time: 20.8 us -> none  [the longest x1 18.1 us: entering(): return lax.fori_loop(0, place, one, state)]
    dot_general x14 -> x0, matrix products: 17.9 us -> none  [the longest x1 3.59 us: local(): inner_sum = jnp.dot(piece, inner_rows, preferred_element_type=jnp.float32)]
    unnamed x1 -> x0, blocking collectives: 11.9 us -> none
  transfers between devices with their start and end apart: 5 -> 0, of which waited for: 2 -> 0; matrix products, arithmetic and copies ran while one was open for 3% -> 0% of each run, Pallas kernels for 0% -> 0%
where the time goes in v1:
time: 87.4 us; the launch traced here: 86.9 us
  Pallas kernels  77.3 us (88%)
  local copies, waits for them, and re-layouts  9.66 us (11%)
    pallas_call x1, Pallas kernels, local(): pl.pallas_call(kernel, out_shape=jax.ShapeDtypeStruct((16, DEPTH), BF16),...  77.3 us
    unnamed x13, local copies, waits for them, and re-layouts  6.79 us

profile of v1, /device:TPU:25, one launch (start us, length us, event | category | flops | bytes accessed | tf_op | source)
XLA Modules:
  0.0 86.9 jit_solution(2817370827081526810)
XLA Ops:
  0.0 0.7 broadcast_in_dim.13
  0.7 0.1 broadcast_in_dim_reshape.3
  0.8 0.7 pad_bitcast_fusion
  1.5 0.7 concatenate.3.small_hbm
  2.2 0.7 pad.13.tapbc_ref
  2.9 0.0 copy-start
  2.9 1.5 %copy-done = bf16[2,3584,128]{2,1,0:T(8,128)(2,1)S(1)} copy-done((bf16[2,3584,128]{2,1,0:T(8,128)(2,1)S(1)}, bf16[2,3584,128]{2,1,0:T(8,128)(2,1)}, u32[]{:S(2)}) %copy-start) | copy-done | bytes 1835032
  4.4 0.0 copy-start.1
  4.4 1.2 %copy-done.1 = bf16[3584,128]{1,0:T(8,128)(2,1)S(1)} copy-done((bf16[3584,128]{1,0:T(8,128)(2,1)S(1)}, bf16[3584,128]{1,0:T(8,128)(2,1)}, u32[]{:S(2)}) %copy-start.1) | copy-done | bytes 917528
  5.5 0.0 copy-start.2
  5.6 1.2 %copy-done.2 = bf16[128,3584]{1,0:T(8,128)(2,1)S(1)} copy-done((bf16[128,3584]{1,0:T(8,128)(2,1)S(1)}, bf16[128,3584]{1,0:T(8,128)(2,1)}, u32[]{:S(2)}) %copy-start.2) | copy-done | bytes 917528
  6.7 0.0 copy-start.3
  6.7 0.9 %copy-done.3 = bf16[512,112]{0,1:T(8,128)(2,1)S(1)} copy-done((bf16[512,112]{0,1:T(8,128)(2,1)S(1)}, bf16[512,112]{0,1:T(8,128)(2,1)}, u32[]{:S(2)}) %copy-start.3) | copy-done | bytes 114712
  7.6 0.0 copy-start.4
  7.6 0.7 copy-done.4
  8.3 0.0 copy-start.5
  8.3 0.7 copy-done.5
  9.0 77.3 %shard_map.118 = bf16[16,3584]{1,0:T(8,128)(2,1)S(1)} custom-call(bf16[112,512]{1,0:T(8,128)(2,1)S(1)} %bitcast.8, bf16[2,3584,128]{2,1,0:T(8,128)(2,1)S(1)} %copy-done, bf16[3584,128]{1,0:T(8,128)(2,1)S(1)} %copy-done.1, bf16[2,3584]{1,0:T(2,128)(2,1)S(1)} %bitcast.9, f32[8,128]{1,0:T(8,128)S(1)} %concatenate.3.small_hbm, f32[8,128]{1,0:T(8,128)S(1)} %pad.13.tapbc_ref, ...), custom_call_target="tpu_custom_call" | custom-call | flops 1879048192 | bytes 10000000 | tf_op jit(solution)/shard_map/pallas_call | solution.py:597
  86.3 0.6 copy.14
Async XLA Ops:
  2.9 1.5 %copy-start = (bf16[2,3584,128]{2,1,0:T(8,128)(2,1)S(1)}, bf16[2,3584,128]{2,1,0:T(8,128)(2,1)}, u32[]{:S(2)}) copy-start(bf16[2,3584,128]{2,1,0:T(8,128)(2,1)} %wzx_hbm.1) | copy-start | bytes 5505028
  4.4 1.2 %copy-start.1 = (bf16[3584,128]{1,0:T(8,128)(2,1)S(1)}, bf16[3584,128]{1,0:T(8,128)(2,1)}, u32[]{:S(2)}) copy-start(bf16[3584,128]{1,0:T(8,128)(2,1)} %wbc_hbm.1) | copy-start | bytes 2752516
  5.5 1.2 %copy-start.2 = (bf16[128,3584]{1,0:T(8,128)(2,1)S(1)}, bf16[128,3584]{1,0:T(8,128)(2,1)}, u32[]{:S(2)}) copy-start(bf16[128,3584]{1,0:T(8,128)(2,1)} %wout_hbm.1) | copy-start | bytes 2752516
  6.7 0.9 %copy-start.3 = (bf16[512,112]{0,1:T(8,128)(2,1)S(1)}, bf16[512,112]{0,1:T(8,128)(2,1)}, u32[]{:S(2)}) copy-start(bf16[512,112]{0,1:T(8,128)(2,1)} %param.12) | copy-start | bytes 344068
  7.6 0.7 copy-start.4
  8.3 0.7 copy-start.5

commit v2 on v1

--- a/solution.py
+++ b/solution.py
@@ -46,9 +46,10 @@
 
 
 def kernel(
-    tok_hbm, wzx_hbm, wbc_hbm, wdt_hbm, small_hbm, tapbc_ref, wout_hbm, seg_hbm,
+    tok_hbm, wzx_hbm, wbc_hbm, wdt_hbm, tap_hbm, gain_hbm, bias_hbm, rate_hbm, skip_hbm, tapbc_hbm,
+    wout_hbm, seg_hbm,
     out_ref,
-    G, WZ, WB, WD, SM, SEG, WO, ACC, LT, HXS, HXR, STS, STR, GN, PS,
+    G, WZ, WB, WD, TAP, GAIN, BIAS, RATE, SKIP, TBC, SEG, WO, ACC, LT, HXS, HXR, STS, STR, GN, PS,
     RXF, RXC, RXS, RZF, RZC, RZS, FS, FR,
     SS, RG, RW, RO, RM, RH, RS, RN, RF, RC, RX, RZ, LC,
 ):
@@ -129,7 +130,11 @@
     l_tok = pltpu.make_async_copy(tok_hbm, gslot(own_f), LC.at[2])
     l_wz = pltpu.make_async_copy(wzx_hbm, WZ, LC.at[3])
     l_wd = pltpu.make_async_copy(wdt_hbm, WD, LC.at[4])
-    l_sm = pltpu.make_async_copy(small_hbm, SM, LC.at[5])
+    l_tb = pltpu.make_async_copy(tapbc_hbm, TBC, LC.at[5])
+    smalls = (
+        (tap_hbm, TAP), (gain_hbm, GAIN), (bias_hbm, BIAS), (rate_hbm, RATE), (skip_hbm, SKIP)
+    )
+    l_sm = [pltpu.make_async_copy(a, v, LC.at[7 + i]) for i, (a, v) in enumerate(smalls)]
     l_sg = pltpu.make_async_copy(seg_hbm, SEG, LC.at[6])
 
     @pl.when(native)
@@ -138,8 +143,10 @@
         l_sg.start()
         l_wz.start()
         l_wd.start()
-        l_sm.start()
-
+        for cp in l_sm:
+            cp.start()
+
+    l_tb.start()
     l_wb.start()
     l_wo.start()
 
@@ -159,7 +166,7 @@
         return pl.ds(pl.multiple_of(m4(y + k) * QUART, 128), QUART)
 
     k0 = count[0]
-    count[0] += 4
+    count[0] += 8
 
     def sp_send(k, src, dst, rsem, device):
         return pltpu.make_async_remote_copy(
@@ -172,7 +179,9 @@
     s_seg = sp_send(0, seg_hbm, SEG, RM.at[2], core)
     s_wz = sp_send(1, wzx_hbm.at[:, quart, :], WZ.at[:, quart, :], RW.at[0], twin)
     s_wd = sp_send(2, wdt_hbm, WD, RM.at[0], twin)
-    s_sm = sp_send(3, small_hbm, SM, RM.at[1], twin)
+    s_sm = [
+        sp_send(3 + i, a, v, RM.at[3 + i], twin) for i, (a, v) in enumerate(smalls)
+    ]
 
     @pl.when(foreign)
     def _():
@@ -193,7 +202,8 @@
     @pl.when(native)
     def _():
         s_wd.start()
-        s_sm.start()
+        for cp in s_sm:
+            cp.start()
         s_wz.start()
 
     def pass_x(wj):
@@ -288,17 +298,20 @@
         arrive(WZ.at[0, qrow(2), :], RW.at[3])
         arrive(WZ.at[1, qrow(2), :], RW.at[4])
         arrive(WD, RM.at[0])
-        arrive(SM, RM.at[1])
+        for i, (_, v) in enumerate(smalls):
+            arrive(v, RM.at[3 + i])
         arrive(SEG, RM.at[2])
 
     @pl.when(native)
     def _():
         l_wz.wait()
         l_wd.wait()
-        l_sm.wait()
+        for cp in l_sm:
+            cp.wait()
         l_sg.wait()
 
     l_wb.wait()
+    l_tb.wait()
 
     for i, wj in enumerate((w, w - sgn, w + sgn, w + 2)):
         for xj in range(4):
@@ -342,10 +355,17 @@
         HXR[0:256, :] = jnp.zeros((256, 128), BF16)
         HXR[256:272, :] = jnp.full((16, 128), -1.0, BF16)
 
-    sm = SM[...]
-    smt = jnp.concatenate([sm, jnp.zeros((120, 128), F32)], 0).T
-    step = softplus(dt_raw + smt[0:2, 6:7])
-    logdec = -smt[0:2, 7:8] * step
+    lane = lax.broadcasted_iota(jnp.int32, (1, 128), 1)
+
+    def two_rows(ref):
+        v = ref[...]
+        return jnp.concatenate([v[:, 0:1], v[:, 1:2]], 0)
+
+    skip = SKIP[...]
+    skip_lane = jnp.where(lane < 64, skip[:, 0:1], skip[:, 1:2])
+    smt = jnp.concatenate([TAP[...], GAIN[...], skip_lane, jnp.zeros((122, 128), F32)], 0).T
+    step = softplus(dt_raw + two_rows(BIAS))
+    logdec = -two_rows(RATE) * step
     hi, mid, low = three_parts(logdec)
     pieces = jnp.concatenate(
         [hi.astype(F32), mid.astype(F32), low.astype(F32), jnp.zeros((2, TOK), F32)], 0
@@ -359,7 +379,7 @@
     enter = jnp.where(seg == first_seg, jnp.exp(cum), 0.0)
     colmat = jnp.concatenate([cum, seg, jnp.zeros((125, TOK), F32)], 0).T
 
-    tb = jnp.concatenate([tapbc_ref[...], jnp.zeros((120, 128), F32)], 0).T
+    tb = jnp.concatenate([TBC[...], jnp.zeros((124, 128), F32)], 0).T
 
     def conv(before, now, seg_before, seg_now, taps):
         both = jnp.concatenate([before, now], 1)
@@ -394,7 +414,6 @@
 
     xdt = xin * by_head(step)
     state = dot_nt(bt, (xdt * by_head(tail)).astype(BF16))
-    lane = lax.broadcasted_iota(jnp.int32, (1, 128), 1)
     tot_lane = jnp.where(lane < 64, total[0:1], total[1:2])
     hi, mid, low = three_parts(tot_lane)
     STS[0:64, :] = state.astype(BF16)
@@ -559,7 +578,8 @@
         s_seg.wait_send()
         s_wz.wait_send()
         s_wd.wait_send()
-        s_sm.wait_send()
+        for cp in s_sm:
+            cp.wait_send()
         o_first.wait_send()
 
     @pl.when(foreign)
@@ -584,27 +604,25 @@
 def local(
     tokens, w_zx, w_bc, w_dt, dt_bias, a_rate, d_skip, conv_x, conv_bc, norm_gain, w_out, segments
 ):
-    def wide(v):
-        return jnp.pad(v, (0, 126))[None]
-
-    small = jnp.concatenate(
-        [conv_x, norm_gain[None], jnp.repeat(d_skip, 64)[None], wide(dt_bias), wide(a_rate)], 0
-    )
-    tapbc = jnp.pad(conv_bc, ((0, 4), (0, 0)))
-    anywhere = pl.BlockSpec(memory_space=pl.ANY)
+    outside = pl.BlockSpec(memory_space=pltpu.HBM)
     inside = pl.BlockSpec(memory_space=pltpu.VMEM)
     dma = pltpu.SemaphoreType.DMA
     return pl.pallas_call(
         kernel,
         out_shape=jax.ShapeDtypeStruct((16, DEPTH), BF16),
-        in_specs=[anywhere] * 5 + [inside] + [anywhere] * 2,
+        in_specs=[outside] * 12,
         out_specs=inside,
         scratch_shapes=[
             pltpu.VMEM((DEPTH, TOK), BF16),
             pltpu.VMEM((2, DEPTH, 128), BF16),
             pltpu.VMEM((DEPTH, 128), BF16),
             pltpu.VMEM((2, DEPTH), BF16),
-            pltpu.VMEM((8, 128), F32),
+            pltpu.VMEM((4, 128), F32),
+            pltpu.VMEM((1, 128), F32),
+            pltpu.VMEM((1, 2), F32),
+            pltpu.VMEM((1, 2), F32),
+            pltpu.VMEM((1, 2), F32),
+            pltpu.VMEM((4, 128), F32),
             pltpu.VMEM((1, TOK), jnp.int32),
             pltpu.VMEM((256, DEPTH), BF16),
             pltpu.VMEM((384, TOK), F32),
@@ -627,7 +645,7 @@
             dma((32,)),
             dma((5,)),
             dma((6,)),
-            dma((3,)),
+            dma((8,)),
             dma((1,)),
             dma((7,)),
             dma((1,)),
@@ -635,15 +653,18 @@
             dma((1,)),
             dma((3, 4)),
             dma((3,)),
-            dma((7,)),
+            dma((12,)),
         ],
         compiler_params=pltpu.CompilerParams(
-            collective_id=0, has_side_effects=True, vmem_limit_bytes=48 * 1024 * 1024
+            collective_id=0, has_side_effects=True, vmem_limit_bytes=60 * 1024 * 1024
         ),
         cost_estimate=pl.CostEstimate(
             flops=2 * TOK * DEPTH * 512, bytes_accessed=10_000_000, transcendentals=500_000
         ),
-    )(tokens.T, w_zx, w_bc, w_dt.T, small, tapbc, w_out, segments.reshape(1, TOK))
+    )(
+        tokens.T, w_zx, w_bc, w_dt.T, conv_x, norm_gain.reshape(1, 128), dt_bias.reshape(1, 2),
+        a_rate.reshape(1, 2), d_skip.reshape(1, 2), conv_bc, w_out, segments.reshape(1, TOK),
+    )
 
 
 def solution(mesh):

time: 87.4 us -> 79.9 us (0.914)
  local copies, waits for them, and re-layouts: 9.66 us -> 1.55 us
  Pallas kernels: 77.3 us -> 78.2 us
    unnamed x13 -> x1, local copies, waits for them, and re-layouts: 6.79 us -> 1.55 us
    broadcast_in_dim x2 -> x0, local copies, waits for them, and re-layouts: 1.4 us -> none  [the longest x1 0.72 us: local(): jnp.repeat(d_skip, 64)[None]]
    pallas_call x1, Pallas kernels: 77.3 us -> 78.2 us  [local(): pl.pallas_call(kernel, out_shape=jax.ShapeDtypeStruct((16, DEPTH), BF16),...]
where the time goes in v2:
time: 79.9 us; the launch traced here: 79.8 us
  Pallas kernels  78.2 us (98%)
  local copies, waits for them, and re-layouts  1.55 us (2%)
    pallas_call x1, Pallas kernels, local(): pl.pallas_call(kernel, out_shape=jax.ShapeDtypeStruct((16, DEPTH), BF16),...  78.2 us

profile of v2, /device:TPU:25, one launch (start us, length us, event | category | flops | bytes accessed | tf_op | source)
XLA Modules:
  0.0 79.8 jit_solution(8588019714539046057)
XLA Ops:
  0.0 78.2 %shard_map.118 = bf16[16,3584]{1,0:T(8,128)(2,1)} custom-call(bf16[112,512]{1,0:T(8,128)(2,1)} %bitcast.7, bf16[2,3584,128]{2,1,0:T(8,128)(2,1)} %wzx_hbm.1, bf16[3584,128]{1,0:T(8,128)(2,1)} %wbc_hbm.1, bf16[2,3584]{1,0:T(2,128)(2,1)} %bitcast.8, f32[4,128]{1,0:T(4,128)} %tap_hbm.1, f32[1,128]{1,0:T(1,128)} %bitcast.10, f32[1,2]{1,0:T(1,128)} %bitcast.11, ...), custom_call_target="tpu_custom_call" | custom-call | flops 1879048192 | bytes 10000000 | tf_op jit(solution)/shard_map/pallas_call | solution.py:610
  78.3 1.6 %copy.14 = bf16[16,3584]{1,0:T(8,128)(2,1)} copy(bf16[16,3584]{1,0:T(8,128)(2,1)} %shard_map.118) | data formatting | bytes 229376
